TPU v7x, 256 devices: a whole 4x4x8 slice. The times are simulated.
256 devices in a mesh: blk: 16 (over z, x_hi), leaf: 8 (over y, core), rhs: 2 (over x_lo).
Axes of the slice: x: 4 (x_hi: 2, x_lo: 2; x = x_hi * 2 + x_lo), y: 4, z: 8, core: 2. Of those that a mesh axis runs over, the one named last changes fastest.
Arguments:
- residual: float32 [32, 8, 65536], P('rhs', 'leaf', 'blk'), may hold values from -160 to 160
- points: float32 [3, 8, 65536], P(None, 'leaf', 'blk'), may hold values from -12330 to 12330
- noise: float32 [8, 65536], P('leaf', 'blk'), may hold values from 1 to 2
- block_list: int32 [8, 8, 256], P('leaf'), may hold values from 0 to 1, as said below
Outputs:
- correction: float32 [32, 8, 65536], P('rhs', 'leaf', 'blk')
- new_residual: float32 [32, 8, 65536], P('rhs', 'leaf', 'blk')
- basis: float32 [128, 8, 65536], P('rhs', 'leaf', 'blk')
Inputs may be any that keep to these rules, and one draw needn't show every extreme that they name: The list is symmetric: block_list[t, k, i] == block_list[t, 7 - k, (i + d) mod 256] with d the offset of entry k.
All inputs are finite; a program needn't handle non-finite values.
Results may differ from a plain program's by a relative error of at most 0.007.
Values sent between devices are 32-bit elements; how exact they have to be, the bound alone decides.
A program may use at most 128 MiB of HBM per device.

v0:
```python
import jax
import jax.numpy as jnp
from jax import lax
from jax.sharding import PartitionSpec as P

M = 32
S = 4
BS = 256
REACH = 4
SUPPORT = 1408
centre_shift = 1.5
amplitude = 1.1
exact = lax.Precision.HIGHEST


def extended(x, sides, width):
    for axis, dim in sides:
        count, length = (lax.axis_size(axis), x.shape[dim])
        up = [(i, (i + 1) % count) for i in range(count)]
        down = [(j, i) for i, j in up]
        last = lax.slice_in_dim(x, length - width, length, axis=dim)
        leading = lax.slice_in_dim(x, 0, width, axis=dim)
        before = lax.ppermute(last, axis, up)
        after = lax.ppermute(leading, axis, down)
        x = jnp.concatenate([before, x, after], axis=dim)
    return x


def kernel_tile(near_points, own_points):
    squared = (near_points[0][:, None] - own_points[0][None, :]) ** 2
    squared = squared + (near_points[1][:, None] - own_points[1][None, :]) ** 2
    squared = squared + (near_points[2][:, None] - own_points[2][None, :]) ** 2
    radius = jnp.sqrt(squared) / SUPPORT
    remain = jnp.maximum(1.0 - radius, 0.0)
    return remain * remain * (remain * remain) * (4.0 * radius + 1.0) * (amplitude / SUPPORT)


def band_product(field_wide, points_wide, weights, rows_out):
    per_turn = rows_out // 8
    count = field_wide.shape[0]

    def turn(carry, index):
        pieces = []
        for inner in range(per_turn):
            block = index * per_turn + inner
            own_points = lax.dynamic_slice_in_dim(points_wide, (block + REACH) * BS, BS, 1)
            total = jnp.zeros((count, BS), jnp.float32)
            for offset in range(2 * REACH + 1):
                column_at = (block + offset) * BS
                near_points = lax.dynamic_slice_in_dim(points_wide, column_at, BS, 1)
                near_field = lax.dynamic_slice_in_dim(field_wide, column_at, BS, 1)
                listed = lax.dynamic_index_in_dim(weights[offset], block, 0, False)
                tile = kernel_tile(near_points, own_points) * listed
                total = total + jnp.dot(near_field, tile, precision=exact)
            pieces.append(total)
        return (carry, jnp.concatenate(pieces, axis=1))

    carry, parts = lax.scan(turn, jnp.zeros((), jnp.int32), jnp.arange(8, dtype=jnp.int32))
    return jnp.moveaxis(parts, 0, 1).reshape(count, rows_out * BS)


def galerkin(gram, count_points, count_sides):
    normed = gram / count_points
    basis_count = normed.shape[0] - count_sides
    gram_basis = normed[:basis_count, :basis_count]
    factor_low = jnp.linalg.cholesky(gram_basis)
    inverse_low = lax.linalg.triangular_solve(
        factor_low, jnp.eye(basis_count, dtype=jnp.float32), left_side=True, lower=True
    )
    cross = normed[:basis_count, count_sides:] + centre_shift * gram_basis
    projected = jnp.dot(
        jnp.dot(inverse_low, cross, precision=exact), inverse_low.T, precision=exact
    )
    projected = 0.5 * (projected + projected.T)
    small_side = jnp.dot(inverse_low, gram_basis[:, :count_sides], precision=exact)
    proj_factor = jnp.linalg.cholesky(projected)
    halfway = lax.linalg.triangular_solve(proj_factor, small_side, left_side=True, lower=True)
    coeffs = lax.linalg.triangular_solve(
        proj_factor, halfway, left_side=True, lower=True, transpose_a=True
    )
    combo = jnp.dot(coeffs.T, inverse_low, precision=exact)
    return (inverse_low, combo)


def row_products(rows):
    return lax.dot_general(rows, rows, (((1,), (1,)), ((), ())), precision=exact)


def local(residual, points, noise, block_list):
    field = residual[:, 0]
    coords = points[:, 0]
    nugget = noise[0]
    own_rows = field.shape[1]
    own_blocks = own_rows // BS
    first_block = lax.axis_index("blk") * own_blocks
    listed = block_list[0].astype(jnp.float32)
    nine = jnp.concatenate(
        [listed[:REACH], jnp.ones((1, listed.shape[1]), jnp.float32), listed[REACH:]], axis=0
    )
    margin = S * REACH
    wrapped = jnp.concatenate([nine[:, -margin:], nine, nine[:, :margin]], axis=1)
    powers = [field]
    rim = REACH * BS
    coords_wide = extended(coords, (("blk", 1),), rim)
    own_weights = lax.dynamic_slice_in_dim(wrapped, first_block + margin, own_blocks, 1)
    current = field
    for power_step in range(S):
        widened = extended(current, (("blk", 1),), rim)
        current = (
            band_product(widened, coords_wide, own_weights, own_blocks)
            + (nugget - centre_shift) * current
        )
        powers.append(current)
    half_panel = jnp.stack(powers, axis=0)
    count_points = own_rows * lax.axis_size("blk") * lax.axis_size("leaf")
    sides_here = field.shape[0]
    whole = lax.all_gather(half_panel, "rhs", axis=1, tiled=True)
    flat = whole.reshape(-1, own_rows)
    gram = lax.psum(row_products(flat), ("blk", "leaf"))
    inverse_low, combo = galerkin(gram, count_points, M)
    first_rows = flat[: S * M]
    image = flat[M:] + centre_shift * first_rows
    part = lax.axis_index("rhs")
    basis_here = S * M // lax.axis_size("rhs")
    mine_low = lax.dynamic_slice_in_dim(inverse_low, part * basis_here, basis_here, 0)
    mine_combo = lax.dynamic_slice_in_dim(combo, part * sides_here, sides_here, 0)
    correction = jnp.dot(mine_combo, first_rows, precision=exact)
    new_residual = field - jnp.dot(mine_combo, image, precision=exact)
    basis = jnp.dot(mine_low, first_rows, precision=exact)
    return (correction[:, None], new_residual[:, None], basis[:, None])


def solution(mesh):
    placed = (
        P("rhs", "leaf", "blk"),
        P(None, "leaf", "blk"),
        P("leaf", "blk"),
        P("leaf", None, None),
    )
    return jax.shard_map(
        local,
        mesh=mesh,
        in_specs=placed,
        out_specs=(P("rhs", "leaf", "blk"), P("rhs", "leaf", "blk"), P("rhs", "leaf", "blk")),
        check_vma=False,
    )
```

profile of v0, /device:TPU:2, one launch (start us, length us, event | category | flops | bytes accessed | tf_op | source)
XLA Modules:
  0.0 2114.2 jit_solution(17787421845742051918)
XLA Ops:
  8.1 2.2 collective-permute-start.2
  10.3 5.4 collective-permute-start.3
  15.6 1.1 copy.47
  16.9 5.6 collective-permute-start.1
  22.5 1.1 bitcast_dynamic-update-slice_fusion
  25.4 206.0 %while.52 = (s32[]{:T(128)}, f32[8,16,512]{2,1,0:T(8,128)S(1)}, s32[8]{0:T(128)S(1)}, f32[16,6144]{1,0:T(8,128)S(1)}, f32[3,6144]{1,0:T(4,128)S(1)}, /*index=5*/...) while((s32[]{:T(128)}, f32[8,16,512]{2,1,0:T(8,128)S(1)}, ...), condition=%wide.region_1.2_spmd, body=%wide.region_0.1_spmd.sunk | while | flops 246620224 | bytes 1092197 | solution.py:58
  231.9 5.6 collective-permute-start.5
  237.9 1.8 collective-permute-done.4
  239.8 202.8 %while.53 = (s32[]{:T(128)}, f32[8,16,512]{2,1,0:T(8,128)S(1)}, s32[8]{0:T(128)S(1)}, f32[16,6144]{1,0:T(8,128)S(1)}, f32[3,6144]{1,0:T(4,128)S(1)}, /*index=5*/...) while((s32[]{:T(128)}, f32[8,16,512]{2,1,0:T(8,128)S(1)}, ...), condition=%wide.region_3.4_spmd, body=%wide.region_2.3_spmd.sunk | while | flops 246620224 | bytes 1092197 | solution.py:58
  442.8 6.1 collective-permute-start.7
  449.2 1.5 collective-permute-done.6
  450.9 203.8 %while.54 = (s32[]{:T(128)}, f32[8,16,512]{2,1,0:T(8,128)S(1)}, s32[8]{0:T(128)S(1)}, f32[16,6144]{1,0:T(8,128)S(1)}, f32[3,6144]{1,0:T(4,128)S(1)}, /*index=5*/...) while((s32[]{:T(128)}, f32[8,16,512]{2,1,0:T(8,128)S(1)}, ...), condition=%wide.region_5.6_spmd, body=%wide.region_4.5_spmd.sunk | while | flops 246620224 | bytes 1092197 | solution.py:58
  654.8 1.9 collective-permute-start.8
  656.7 4.4 collective-permute-start.9
  661.4 1.8 collective-permute-done.8
  663.4 207.7 %while.55 = (s32[]{:T(128)}, f32[8,16,512]{2,1,0:T(8,128)S(1)}, s32[8]{0:T(128)S(1)}, f32[16,6144]{1,0:T(8,128)S(1)}, f32[3,6144]{1,0:T(4,128)S(1)}, /*index=5*/...) while((s32[]{:T(128)}, f32[8,16,512]{2,1,0:T(8,128)S(1)}, ...), condition=%wide.region_7.8_spmd, body=%wide.region_6.7_spmd.sunk | while | flops 246620224 | bytes 1092197 | solution.py:58
  871.3 1.0 copy-done.4
  872.7 45.1 %all-gather.2.cloned.1.call-done = f32[5,32,4096]{2,1,0:T(8,128)} async-done(((f32[5,16,4096]{2,1,0:T(8,128)}), f32[5,32,4096]{2,1,0:T(8,128)}) %all-gather.2.cloned.1.call-update) | async-done | bytes 2621456 | tf_op jit(solution)/shard_map/all_gather | solution.py:117
  917.8 5.6 fusion.2577
  923.9 1.3 copy-done.1
  925.2 1.6 bitcast_add_fusion
  926.8 1122.0 %all-reduce.2.cloned.1.call-done = f32[160,160]{0,1:T(8,128)} async-done(((f32[160,160]{0,1:T(8,128)}), f32[160,160]{0,1:T(8,128)}) %all-reduce.2.cloned.1.call-update) | async-done | bytes 102416 | tf_op jit(solution)/shard_map/psum | solution.py:119
  2049.9 11.7 cholesky.44
  2062.9 9.8 custom-call.10
  2074.0 12.0 cholesky.55
  2087.3 9.8 custom-call.11
  2097.8 2.7 fusion.2532
  2100.6 1.0 copy.29
  2101.6 1.1 convolution_bitcast_fusion.1
  2102.7 1.2 convolution_bitcast_fusion
  2103.9 2.0 copy.30
  2105.9 1.0 copy.28
  (952 shorter events, 424.7 us)
Async XLA Ops:
  7.2 910.6 %all-gather.2.cloned.1.call-start = ((), (), s32[]{:S(2)}) async-start(), calls=%async_computation | async-start | bytes 3932160 | tf_op jit(solution)/shard_map/all_gather | solution.py:117
  8.1 17.2 collective-permute-start.2
  10.3 15.0 collective-permute-start.3
  16.8 8.5 collective-permute-start
  16.9 8.4 collective-permute-start.1
  25.4 206.0 %copy-start.3 = (f32[16,1,4096]{2,1,0:T(1,128)S(1)}, f32[16,1,4096]{2,1,0:T(1,128)}, u32[]{:S(2)}) copy-start(f32[16,1,4096]{2,1,0:T(1,128)} %param.13) | copy-start | bytes 786436
  231.6 8.2 collective-permute-start.4
  231.9 7.9 collective-permute-start.5
  442.7 8.0 collective-permute-start.6
  442.8 8.0 collective-permute-start.7
  654.8 8.4 collective-permute-start.8
  656.7 6.6 collective-permute-start.9
  871.3 1.1 copy-start.4
  872.4 1176.4 %all-reduce.2.cloned.1.call-start = ((), (), s32[]{:S(2)}) async-start(), calls=%async_computation.1 | async-start | bytes 327680 | tf_op jit(solution)/shard_map/psum | solution.py:119
  917.8 5.6 copy-start
  923.9 1.3 copy-start.1
  2073.9 27.7 %copy-start.2 = (f32[4,32,4096]{2,1,0:T(8,128)S(1)}, f32[4,32,4096]{2,1,0:T(8,128)}, u32[]{:S(2)}) copy-start(f32[4,32,4096]{2,1,0:T(8,128)} %copy-done.1) | copy-start | bytes 6291460
Sparse Core Ops, SparseCore 0:
  872.5 45.1 all-gather.1
  923.5 1125.2 all-reduce.1
where the time goes:
time: 2130 us; the launch traced here: 2110 us
  waiting for transfers between devices  1170 us (55%)
  loops' own time  407 us (19%)
  matrix products  296 us (14%)
  local copies, waits for them, and re-layouts  140 us (7%)
  other arithmetic  51.7 us (2%)
  starting transfers between devices  32 us (2%)
    psum x1, waiting for transfers between devices, local(): gram = lax.psum(row_products(flat), ('blk', 'leaf'))  1120 us
    another operation x4, loops' own time, band_product(): lax.scan(turn, jnp.zeros((), jnp.int32), jnp.arange(8, dtype=jnp.int32))  407 us
    dot_general x576, matrix products, turn(): total = total + jnp.dot(near_field, tile, precision=exact)  284 us
    dynamic_slice x160, local copies, waits for them, and re-layouts, turn(): listed = lax.dynamic_index_in_dim(weights[offset], block, 0, False)  105 us
    all_gather x1, waiting for transfers between devices, local(): whole = lax.all_gather(half_panel, 'rhs', axis=1, tiled=True)  45.1 us
  transfers between devices with their start and end apart: 12, of which 7 were waited for; matrix products, arithmetic and copies ran while one was open for 0% of the time, Pallas kernels for 0%

commit v1 on v0

--- a/solution.py
+++ b/solution.py
@@ -116,7 +116,7 @@
     sides_here = field.shape[0]
     whole = lax.all_gather(half_panel, "rhs", axis=1, tiled=True)
     flat = whole.reshape(-1, own_rows)
-    gram = lax.psum(row_products(flat), ("blk", "leaf"))
+    gram = lax.psum(lax.psum(row_products(flat), "leaf"), "blk")
     inverse_low, combo = galerkin(gram, count_points, M)
     first_rows = flat[: S * M]
     image = flat[M:] + centre_shift * first_rows

time: 2130 us -> 1230 us (0.58)
  waiting for transfers between devices: 1170 us -> 267 us
    psum x1 -> x2, waiting for transfers between devices: 1120 us -> 217 us  [local(): gram = lax.psum(lax.psum(row_products(flat), 'leaf'), 'blk')]
  transfers between devices with their start and end apart: 12 -> 13, of which waited for: 7 -> 8; matrix products, arithmetic and copies ran while one was open for 0% -> 1% of each run, Pallas kernels for 0% -> 0%
where the time goes in v1:
time: 1230 us; the launch traced here: 1220 us
  loops' own time  411 us (33%)
  matrix products  296 us (24%)
  waiting for transfers between devices  267 us (22%)
  local copies, waits for them, and re-layouts  142 us (12%)
  other arithmetic  53.9 us (4%)
  starting transfers between devices  32.1 us (3%)
  between operations  14.7 us (1%)
    another operation x4, loops' own time, band_product(): lax.scan(turn, jnp.zeros((), jnp.int32), jnp.arange(8, dtype=jnp.int32))  411 us
    dot_general x576, matrix products, turn(): total = total + jnp.dot(near_field, tile, precision=exact)  284 us
    psum x2, waiting for transfers between devices, local(): gram = lax.psum(lax.psum(row_products(flat), 'leaf'), 'blk')  217 us
    dynamic_slice x160, local copies, waits for them, and re-layouts, turn(): listed = lax.dynamic_index_in_dim(weights[offset], block, 0, False)  105 us
    all_gather x1, waiting for transfers between devices, local(): whole = lax.all_gather(half_panel, 'rhs', axis=1, tiled=True)  45.3 us
    ppermute x5, starting transfers between devices, extended(): after = lax.ppermute(leading, axis, down)  27.2 us
  transfers between devices with their start and end apart: 13, of which 8 were waited for; matrix products, arithmetic and copies ran while one was open for 1% of the time, Pallas kernels for 0%

profile of v1, /device:TPU:2, one launch (start us, length us, event | category | flops | bytes accessed | tf_op | source)
XLA Modules:
  0.0 1217.0 jit_solution(10102002933254784757)
XLA Ops:
  8.1 2.2 collective-permute-start.2
  10.3 5.4 collective-permute-start.3
  15.6 1.1 copy.47
  16.9 5.6 collective-permute-start.1
  22.5 1.1 bitcast_dynamic-update-slice_fusion
  25.4 204.8 %while.52 = (s32[]{:T(128)}, f32[8,16,512]{2,1,0:T(8,128)S(1)}, s32[8]{0:T(128)S(1)}, f32[16,6144]{1,0:T(8,128)S(1)}, f32[3,6144]{1,0:T(4,128)S(1)}, /*index=5*/...) while((s32[]{:T(128)}, f32[8,16,512]{2,1,0:T(8,128)S(1)}, ...), condition=%wide.region_1.2_spmd, body=%wide.region_0.1_spmd.sunk | while | flops 246620224 | bytes 1092197 | solution.py:58
  230.8 5.6 collective-permute-start.5
  236.8 1.8 collective-permute-done.4
  238.7 205.5 %while.53 = (s32[]{:T(128)}, f32[8,16,512]{2,1,0:T(8,128)S(1)}, s32[8]{0:T(128)S(1)}, f32[16,6144]{1,0:T(8,128)S(1)}, f32[3,6144]{1,0:T(4,128)S(1)}, /*index=5*/...) while((s32[]{:T(128)}, f32[8,16,512]{2,1,0:T(8,128)S(1)}, ...), condition=%wide.region_3.4_spmd, body=%wide.region_2.3_spmd.sunk | while | flops 246620224 | bytes 1092197 | solution.py:58
  444.4 6.1 collective-permute-start.7
  450.8 1.5 collective-permute-done.6
  452.5 208.4 %while.54 = (s32[]{:T(128)}, f32[8,16,512]{2,1,0:T(8,128)S(1)}, s32[8]{0:T(128)S(1)}, f32[16,6144]{1,0:T(8,128)S(1)}, f32[3,6144]{1,0:T(4,128)S(1)}, /*index=5*/...) while((s32[]{:T(128)}, f32[8,16,512]{2,1,0:T(8,128)S(1)}, ...), condition=%wide.region_5.6_spmd, body=%wide.region_4.5_spmd.sunk | while | flops 246620224 | bytes 1092197 | solution.py:58
  661.0 1.9 collective-permute-start.8
  662.9 4.4 collective-permute-start.9
  667.6 1.8 collective-permute-done.8
  669.6 206.8 %while.55 = (s32[]{:T(128)}, f32[8,16,512]{2,1,0:T(8,128)S(1)}, s32[8]{0:T(128)S(1)}, f32[16,6144]{1,0:T(8,128)S(1)}, f32[3,6144]{1,0:T(4,128)S(1)}, /*index=5*/...) while((s32[]{:T(128)}, f32[8,16,512]{2,1,0:T(8,128)S(1)}, ...), condition=%wide.region_7.8_spmd, body=%wide.region_6.7_spmd.sunk | while | flops 246620224 | bytes 1092197 | solution.py:58
  876.7 1.1 copy-done.3
  877.8 45.3 %all-gather.2.cloned.1.call-done = f32[5,32,4096]{2,1,0:T(8,128)} async-done(((f32[5,16,4096]{2,1,0:T(8,128)}), f32[5,32,4096]{2,1,0:T(8,128)}) %all-gather.2.cloned.1.call-update) | async-done | bytes 2621456 | tf_op jit(solution)/shard_map/all_gather | solution.py:117
  923.1 5.6 fusion.2577
  929.0 2.6 fusion.2570
  931.6 62.5 %all-reduce.3.cloned.1.call-done = f32[160,160]{0,1:T(8,128)} async-done(((f32[160,160]{0,1:T(8,128)}), f32[160,160]{0,1:T(8,128)}) %all-reduce.3.cloned.1.call-update) | async-done | bytes 102416 | tf_op jit(solution)/shard_map/psum | solution.py:119
  994.1 3.9 bitcast_add_fusion
  998.0 154.0 %all-reduce.5.cloned.1.call-done = f32[160,160]{0,1:T(8,128)} async-done(((f32[160,160]{0,1:T(8,128)}), f32[160,160]{0,1:T(8,128)}) %all-reduce.5.cloned.1.call-update) | async-done | bytes 102416 | tf_op jit(solution)/shard_map/psum | solution.py:119
  1153.1 11.7 cholesky.44
  1166.1 9.8 custom-call.10
  1177.2 11.7 cholesky.55
  1190.2 10.0 custom-call.11
  1201.0 2.7 fusion.2532
  1203.7 1.0 copy.29
  1204.7 1.1 convolution_bitcast_fusion.1
  1205.8 1.2 convolution_bitcast_fusion
  1207.0 2.0 copy.30
  (953 shorter events, 426.6 us)
Async XLA Ops:
  7.2 916.0 %all-gather.2.cloned.1.call-start = ((), (), s32[]{:S(2)}) async-start(), calls=%async_computation | async-start | bytes 3932160 | tf_op jit(solution)/shard_map/all_gather | solution.py:117
  8.1 17.2 %collective-permute-start.2 = (f32[3,1024]{1,0:T(4,128)S(1)}, f32[3,1024]{1,0:T(4,128)S(1)}, u32[]{:S(2)}, u32[]{:S(2)}) collective-permute-start(f32[3,1024]{1,0:T(4,128)S(1)} %get-tuple-element.898), channel_id=1, source_target_pairs={{0,16},{16,32},{32,48},{48,64},{64,80},{80,96},{96,112},{112,128},... | collective-permute-start | bytes 36872 | tf_op jit(solution)/shard_map/ppermute | solution.py:23
  10.3 15.0 %collective-permute-start.3 = (f32[3,1024]{1,0:T(4,128)S(1)}, f32[3,1024]{1,0:T(4,128)S(1)}, u32[]{:S(2)}, u32[]{:S(2)}) collective-permute-start(f32[3,1024]{1,0:T(4,128)S(1)} %get-tuple-element.899), channel_id=1, source_target_pairs={{16,0},{32,16},{48,32},{64,48},{80,64},{96,80},{112,96},{128,112},... | collective-permute-start | bytes 36872 | tf_op jit(solution)/shard_map/ppermute | solution.py:24
  16.8 8.5 collective-permute-start
  16.9 8.4 collective-permute-start.1
  25.4 204.9 %copy-start.2 = (f32[16,1,4096]{2,1,0:T(1,128)S(1)}, f32[16,1,4096]{2,1,0:T(1,128)}, u32[]{:S(2)}) copy-start(f32[16,1,4096]{2,1,0:T(1,128)} %param.13) | copy-start | bytes 786436
  230.5 8.2 collective-permute-start.4
  230.8 7.9 collective-permute-start.5
  444.3 8.0 collective-permute-start.6
  444.4 8.0 collective-permute-start.7
  661.0 8.4 collective-permute-start.8
  662.9 6.6 collective-permute-start.9
  876.7 1.1 copy-start.3
  877.8 116.3 %all-reduce.3.cloned.1.call-start = ((), (), s32[]{:S(2)}) async-start(), calls=%async_computation.1 | async-start | bytes 327680 | tf_op jit(solution)/shard_map/psum | solution.py:119
  923.1 5.9 copy-start
  928.8 223.2 %all-reduce.5.cloned.1.call-start = ((), (), s32[]{:S(2)}) async-start(), calls=%async_computation.2 | async-start | bytes 327680 | tf_op jit(solution)/shard_map/psum | solution.py:119
  1177.1 27.7 %copy-start.1 = (f32[4,32,4096]{2,1,0:T(8,128)S(1)}, f32[4,32,4096]{2,1,0:T(8,128)}, u32[]{:S(2)}) copy-start(f32[4,32,4096]{2,1,0:T(8,128)} %get-tuple-element.889) | copy-start | bytes 6291460
Sparse Core Ops, SparseCore 0:
  877.9 45.1 all-gather.1
  928.9 65.1 all-reduce.2
  996.9 155.0 all-reduce.4
